TPU v7x, 32 devices: a whole 2x2x4 slice. The times are simulated.
32 devices in a mesh: phase: 16 (over z, y, x), lat: 2 (over core).
Axes of the slice: x: 2, y: 2, z: 4, core: 2. Of those that a mesh axis runs over, the one named last changes fastest.
Arguments:
- state_now: float32 [3, 64, 1024], P(None, ('lat', 'phase')), may hold values from -4 to 4
- ocean_depth: float32 [64, 1024], P('lat'), may hold values from 0.5 to 1.5
- coriolis: float32 [64], P('lat'), may hold values from -0.4 to 0.4
- phase_times: float32 [16], P('phase'), may hold values from -6 to 6
- phase_weights: float32 [16], P('phase'), may hold values from 0.00625 to 0.25
Outputs:
- state_next: float32 [3, 64, 1024], P(None, ('lat', 'phase'))
- tendency: float32 [3, 64, 1024], P(None, ('lat', 'phase'))
All inputs are finite; a program needn't handle non-finite values.
Results may differ from a plain program's by a relative error of at most 0.00002.
Values sent between devices are 32-bit elements; how exact they have to be, the bound alone decides.
A program may use at most 64 MiB of HBM per device.

v0:
```python
import math
import jax
import jax.numpy as jnp
from jax import lax
from jax.sharding import PartitionSpec as P

DEG = 8
DEPTH = 4
radius_scale = 2.5
time_step = 0.5
series_terms = 20


def extended(shard, sides, width):
    for axis, dim in sides:
        devices, length = (lax.axis_size(axis), shard.shape[dim])
        up = [(i, (i + 1) % devices) for i in range(devices - 1)]
        down = [(j, i) for i, j in up]
        last = lax.slice_in_dim(shard, length - width, length, axis=dim)
        first = lax.slice_in_dim(shard, 0, width, axis=dim)
        before = lax.ppermute(last, axis, up)
        after = lax.ppermute(first, axis, down)
        shard = jnp.concatenate([before, shard, after], axis=dim)
    return shard


def along_lon(values):
    return (jnp.roll(values, -1, axis=-1) - jnp.roll(values, 1, axis=-1)) * 0.5


def along_lat(values):
    return (values[..., 2:, :] - values[..., :-2, :]) * 0.5


def interior(values):
    return values[..., 1:-1, :]


def wave_operator(fields, coefficients):
    height = fields[:, 0]
    eastward = fields[:, 1]
    northward = fields[:, 2]
    depth_field = coefficients[0]
    rotation = coefficients[1]
    out_height = -(along_lon(interior(depth_field * eastward)) + along_lat(depth_field * northward))
    out_east = -along_lon(interior(height)) + interior(rotation * northward)
    out_north = -along_lat(height) - interior(rotation * eastward)
    return jnp.stack([out_height, out_east, out_north], axis=1) / radius_scale


def advection(fields):
    height = fields[:, 0]
    eastward = fields[:, 1]
    northward = fields[:, 2]
    mid_east = interior(eastward)
    mid_north = interior(northward)
    out_height = -(along_lon(interior(height * eastward)) + along_lat(height * northward))
    out_east = -(mid_east * along_lon(mid_east) + mid_north * along_lat(eastward))
    out_north = -(mid_east * along_lon(mid_north) + mid_north * along_lat(northward))
    return jnp.stack([out_height, out_east, out_north], axis=1)


def series_coeffs(sample_time):
    half_time = sample_time * 0.5
    square = half_time * half_time
    result = []
    for degree in range(DEG + 1):
        summed = jnp.zeros_like(sample_time)
        term_sq = jnp.ones_like(sample_time)
        for series in range(series_terms):
            factor = (-1.0) ** series / (math.factorial(series) * math.factorial(series + degree))
            summed = summed + factor * term_sq
            term_sq = term_sq * square
        result.append(summed * half_time**degree)
    return result


def trimmed(values, have, wanted):
    excess = have - wanted
    if excess == 0:
        return values
    return values[:, :, excess : values.shape[2] - excess]


def per_device(state_now, ocean_depth, coriolis, phase_times, phase_weights):
    tile_rows = ocean_depth.shape[0]
    lat_count = lax.axis_size("lat")
    lat_place = lax.axis_index("lat")
    stacked = jnp.stack([ocean_depth, jnp.broadcast_to(coriolis[:, None], ocean_depth.shape)])
    coefficients = extended(stacked, (("lat", 1),), DEPTH)
    global_rows = lat_place * tile_rows - DEPTH + jnp.arange(tile_rows + 2 * DEPTH, dtype=jnp.int32)
    inside = ((global_rows >= 0) & (global_rows < tile_rows * lat_count)).astype(jnp.float32)
    forward = series_coeffs(phase_times)
    backward = series_coeffs(-phase_times)
    sample_count = phase_times.shape[0]

    def band_coeffs(margin):
        return coefficients[:, DEPTH - margin : DEPTH + tile_rows + margin]

    def band_inside(margin):
        return inside[DEPTH - margin : DEPTH + tile_rows + margin][None, None, :, None]

    def exponential(fields, series):
        accumulated = series[0][:, None, None, None] * fields
        previous = None
        current = fields
        width_prev = 0
        width_cur = 0
        for degree in range(1, DEG + 1):
            if (degree - 1) % DEPTH == 0:
                if previous is None:
                    current = extended(current, (("lat", 2),), DEPTH)
                else:
                    joined = jnp.concatenate(
                        [trimmed(previous, width_prev, 0), trimmed(current, width_cur, 0)], axis=0
                    )
                    joined = extended(joined, (("lat", 2),), DEPTH)
                    previous = joined[:sample_count]
                    current = joined[sample_count:]
                    width_prev = DEPTH
                width_cur = DEPTH
            width_new = width_cur - 1
            applied = wave_operator(current, band_coeffs(width_cur))
            if previous is None:
                advanced = applied
            else:
                advanced = 2.0 * applied + trimmed(previous, width_prev, width_new)
            advanced = advanced * band_inside(width_new)
            accumulated = accumulated + 2.0 * series[degree][:, None, None, None] * trimmed(
                advanced, width_new, 0
            )
            previous = current
            width_prev = width_cur
            current = advanced
            width_cur = width_new
        return accumulated

    def averaged(whole_tile):
        samples = whole_tile[None]
        waves = exponential(samples, forward)
        rimmed = extended(waves, (("lat", 2),), 1)
        pulled = advection(rimmed)
        returned = exponential(pulled, backward)
        return jnp.sum(phase_weights[:, None, None, None] * returned, axis=0)

    whole_tile = lax.all_gather(state_now, "phase", axis=1, tiled=True)

    def summed_whole(partial_value):
        return lax.psum(partial_value, "phase")

    first = summed_whole(averaged(whole_tile))
    middle = whole_tile + time_step * first
    second = summed_whole(averaged(middle))
    tendency_tile = 0.5 * (first + second)
    share = state_now.shape[1]
    start = lax.axis_index("phase") * share
    tendency = lax.dynamic_slice_in_dim(tendency_tile, start, share, 1)
    state_next = state_now + time_step * tendency
    return (state_next, tendency)


def solution(mesh):
    placed = (P(None, ("lat", "phase"), None), P("lat", None), P("lat"), P("phase"), P("phase"))
    return jax.shard_map(
        per_device,
        mesh=mesh,
        in_specs=placed,
        out_specs=(P(None, ("lat", "phase"), None), P(None, ("lat", "phase"), None)),
        check_vma=False,
    )
```

profile of v0, /device:TPU:0, one launch (start us, length us, event | category | flops | bytes accessed | tf_op | source)
XLA Modules:
  0.0 368.3 jit_solution(13352655160559666389)
XLA Ops:
  7.2 0.8 copy.168
  8.0 45.3 %all_gather.3 = f32[3,32,1024]{2,0,1:T(4,128)S(1)} all-gather(f32[3,2,1024]{2,0,1:T(4,128)S(1)} %copy.168), channel_id=1, replica_groups=mesh['phase'=16,'lat'=2] {'phase'}, dimensions={1}, use_global_device_ids=true | all-gather | bytes 417792 | tf_op jit(solution)/shard_map/all_gather | solution.py:146
  53.3 0.2 copy.179
  53.6 1.4 collective-permute-start.3
  55.0 3.0 collective-permute-start.2
  58.2 1.3 collective-permute-start.1
  59.5 3.0 collective-permute-start
  62.8 0.5 collective-permute-done
  64.0 0.2 fusion.311
  67.0 1.3 collective-permute-start.5
  68.3 3.0 collective-permute-start.4
  73.0 0.2 pad_maximum_fusion
  73.9 0.1 fusion.271
  74.1 0.1 fusion.16
  74.8 0.1 fusion.261
  75.8 0.7 fusion.49
  76.5 1.3 collective-permute-start.7
  77.8 3.0 collective-permute-start.6
  80.9 0.8 collective-permute-done.6
  82.5 0.2 fusion.451
  82.7 1.3 collective-permute-start.9
  84.0 3.0 collective-permute-start.8
  87.1 0.9 collective-permute-done.8
  88.6 0.1 fusion.251
  89.4 0.1 fusion.241
  91.5 1.3 collective-permute-start.11
  92.8 3.2 collective-permute-start.10
  97.5 0.2 pad_maximum_fusion.1
  98.4 0.1 fusion.211
  98.5 0.1 fusion.11
  100.2 1.3 fusion.41
  101.6 104.9 %all-reduce.3.cloned.1.call-done = f32[3,32,1024]{2,1,0:T(8,128)} async-done(((f32[3,32,1024]{2,1,0:T(8,128)}), f32[3,32,1024]{2,1,0:T(8,128)}) %all-reduce.3.cloned.1.call-update) | async-done | bytes 393232 | tf_op jit(solution)/shard_map/psum | solution.py:149
  206.5 1.2 fusion.500
  207.8 1.3 collective-permute-start.13
  209.1 3.0 collective-permute-start.12
  212.1 0.9 collective-permute-done.12
  214.5 0.1 fusion.181
  215.4 0.1 fusion.171
  215.5 0.1 fusion.8
  216.6 1.3 collective-permute-start.15
  217.9 3.0 collective-permute-start.14
  220.9 0.9 collective-permute-done.14
  222.6 0.2 pad_maximum_fusion.2
  223.5 0.1 fusion.151
  223.6 0.1 fusion.6
  224.4 0.1 fusion.141
  224.5 0.1 fusion.5
  225.4 0.9 copy-done
  226.2 0.7 fusion.31
  227.0 1.3 collective-permute-start.17
  228.3 3.0 collective-permute-start.16
  231.3 0.8 collective-permute-done.16
  232.9 0.2 fusion.397
  233.2 1.3 collective-permute-start.19
  234.5 3.3 collective-permute-start.18
  237.8 0.6 collective-permute-done.18
  241.9 1.3 collective-permute-start.21
  243.2 3.0 collective-permute-start.20
  246.3 0.9 collective-permute-done.20
  247.9 0.2 pad_maximum_fusion.3
  249.0 0.1 fusion.1
  250.7 1.3 fusion.23
  252.0 107.9 %all-reduce.5.cloned.1.call-done = f32[3,32,1024]{2,1,0:T(8,128)} async-done(((f32[3,32,1024]{2,1,0:T(8,128)}), f32[3,32,1024]{2,1,0:T(8,128)}) %all-reduce.5.cloned.1.call-update) | async-done | bytes 393232 | tf_op jit(solution)/shard_map/psum | solution.py:149
  359.9 1.5 multiply_add_fusion.1
  (340 shorter events, 26.2 us)
Async XLA Ops:
  7.2 199.3 %all-reduce.3.cloned.1.call-start = ((), (), s32[]{:S(2)}) async-start(), calls=%async_computation | async-start | bytes 786432 | tf_op jit(solution)/shard_map/psum | solution.py:149
  53.5 4.6 %copy-start.1 = (f32[32,1024]{1,0:T(8,128)S(1)}, f32[32,1024]{1,0:T(8,128)}, u32[]{:S(2)}) copy-start(f32[32,1024]{1,0:T(8,128)} %param.6) | copy-start | bytes 393220
  53.6 4.5 %copy-start.3 = (f32[32]{0:T(128)S(1)}, f32[32]{0:T(128)}, u32[]{:S(2)}) copy-start(f32[32]{0:T(128)} %param.7) | copy-start | bytes 388
  53.6 9.8 %collective-permute-start.3 = (f32[1,3,4,1024]{3,2,1,0:T(4,128)S(1)}, f32[1,3,4,1024]{3,2,1,0:T(4,128)S(1)}, u32[]{:S(2)}, u32[]{:S(2)}) collective-permute-start(f32[1,3,4,1024]{3,2,1,0:T(4,128)S(1)} %get-tuple-element.195), channel_id=1, source_target_pairs={{1,0},{3,2},{5,4},{7,6},{9,8},{11,10},{13,12},{15,14},{17,16},{19,... | collective-permute-start | bytes 147464 | tf_op jit(solution)/shard_map/ppermute | solution.py:22
  55.0 8.4 %collective-permute-start.2 = (f32[1,3,4,1024]{3,2,1,0:T(4,128)S(1)}, f32[1,3,4,1024]{3,2,1,0:T(4,128)S(1)}, u32[]{:S(2)}, u32[]{:S(2)}) collective-permute-start(f32[1,3,4,1024]{3,2,1,0:T(4,128)S(1)} %get-tuple-element.194), channel_id=1, source_target_pairs={{0,1},{2,3},{4,5},{6,7},{8,9},{10,11},{12,13},{14,15},{16,17},{18,... | collective-permute-start | bytes 147464 | tf_op jit(solution)/shard_map/ppermute | solution.py:21
  58.2 4.6 %collective-permute-start.1 = (f32[2,4,1024]{2,1,0:T(4,128)S(1)}, f32[2,4,1024]{2,1,0:T(4,128)S(1)}, u32[]{:S(2)}, u32[]{:S(2)}) collective-permute-start(f32[2,4,1024]{2,1,0:T(4,128)S(1)} %get-tuple-element.205), channel_id=1, source_target_pairs={{1,0},{3,2},{5,4},{7,6},{9,8},{11,10},{13,12},{15,14},{17,16},{19,... | collective-permute-start | bytes 98312 | tf_op jit(solution)/shard_map/ppermute | solution.py:22
  59.5 3.9 %collective-permute-start = (f32[2,4,1024]{2,1,0:T(4,128)S(1)}, f32[2,4,1024]{2,1,0:T(4,128)S(1)}, u32[]{:S(2)}, u32[]{:S(2)}) collective-permute-start(f32[2,4,1024]{2,1,0:T(4,128)S(1)} %get-tuple-element.204), channel_id=1, source_target_pairs={{0,1},{2,3},{4,5},{6,7},{8,9},{10,11},{12,13},{14,15},{16,17},{18,... | collective-permute-start | bytes 98312 | tf_op jit(solution)/shard_map/ppermute | solution.py:21
  67.0 5.3 %collective-permute-start.5 = (f32[2,3,4,1024]{3,2,1,0:T(4,128)S(1)}, f32[2,3,4,1024]{3,2,1,0:T(4,128)S(1)}, u32[]{:S(2)}, u32[]{:S(2)}) collective-permute-start(f32[2,3,4,1024]{3,2,1,0:T(4,128)S(1)} %get-tuple-element.91), channel_id=1, source_target_pairs={{1,0},{3,2},{5,4},{7,6},{9,8},{11,10},{13,12},{15,14},{17,16},{19,... | collective-permute-start | bytes 294920 | tf_op jit(solution)/shard_map/ppermute | solution.py:22
  68.3 4.0 %collective-permute-start.4 = (f32[2,3,4,1024]{3,2,1,0:T(4,128)S(1)}, f32[2,3,4,1024]{3,2,1,0:T(4,128)S(1)}, u32[]{:S(2)}, u32[]{:S(2)}) collective-permute-start(f32[2,3,4,1024]{3,2,1,0:T(4,128)S(1)} %get-tuple-element.90), channel_id=1, source_target_pairs={{0,1},{2,3},{4,5},{6,7},{8,9},{10,11},{12,13},{14,15},{16,17},{18,... | collective-permute-start | bytes 294920 | tf_op jit(solution)/shard_map/ppermute | solution.py:21
  76.5 4.3 %collective-permute-start.7 = (f32[1,3,1,1024]{3,2,1,0:T(1,128)S(1)}, f32[1,3,1,1024]{3,2,1,0:T(1,128)S(1)}, u32[]{:S(2)}, u32[]{:S(2)}) collective-permute-start(f32[1,3,1,1024]{3,2,1,0:T(1,128)S(1)} %get-tuple-element.193), channel_id=1, source_target_pairs={{1,0},{3,2},{5,4},{7,6},{9,8},{11,10},{13,12},{15,14},{17,16},{19,... | collective-permute-start | bytes 36872 | tf_op jit(solution)/shard_map/ppermute | solution.py:22
  77.8 3.9 %collective-permute-start.6 = (f32[1,3,1,1024]{3,2,1,0:T(1,128)S(1)}, f32[1,3,1,1024]{3,2,1,0:T(1,128)S(1)}, u32[]{:S(2)}, u32[]{:S(2)}) collective-permute-start(f32[1,3,1,1024]{3,2,1,0:T(1,128)S(1)} %get-tuple-element.192), channel_id=1, source_target_pairs={{0,1},{2,3},{4,5},{6,7},{8,9},{10,11},{12,13},{14,15},{16,17},{18,... | collective-permute-start | bytes 36872 | tf_op jit(solution)/shard_map/ppermute | solution.py:21
  82.7 4.3 %collective-permute-start.9 = (f32[1,3,4,1024]{3,2,1,0:T(4,128)S(1)}, f32[1,3,4,1024]{3,2,1,0:T(4,128)S(1)}, u32[]{:S(2)}, u32[]{:S(2)}) collective-permute-start(f32[1,3,4,1024]{3,2,1,0:T(4,128)S(1)} %get-tuple-element.191), channel_id=1, source_target_pairs={{1,0},{3,2},{5,4},{7,6},{9,8},{11,10},{13,12},{15,14},{17,16},{19,... | collective-permute-start | bytes 147464 | tf_op jit(solution)/shard_map/ppermute | solution.py:22
  84.0 3.9 %collective-permute-start.8 = (f32[1,3,4,1024]{3,2,1,0:T(4,128)S(1)}, f32[1,3,4,1024]{3,2,1,0:T(4,128)S(1)}, u32[]{:S(2)}, u32[]{:S(2)}) collective-permute-start(f32[1,3,4,1024]{3,2,1,0:T(4,128)S(1)} %get-tuple-element.190), channel_id=1, source_target_pairs={{0,1},{2,3},{4,5},{6,7},{8,9},{10,11},{12,13},{14,15},{16,17},{18,... | collective-permute-start | bytes 147464 | tf_op jit(solution)/shard_map/ppermute | solution.py:21
  91.5 5.2 %collective-permute-start.11 = (f32[2,3,4,1024]{3,2,1,0:T(4,128)S(1)}, f32[2,3,4,1024]{3,2,1,0:T(4,128)S(1)}, u32[]{:S(2)}, u32[]{:S(2)}) collective-permute-start(f32[2,3,4,1024]{3,2,1,0:T(4,128)S(1)} %get-tuple-element.89), channel_id=1, source_target_pairs={{1,0},{3,2},{5,4},{7,6},{9,8},{11,10},{13,12},{15,14},{17,16},{19,... | collective-permute-start | bytes 294920 | tf_op jit(solution)/shard_map/ppermute | solution.py:22
  92.8 4.0 %collective-permute-start.10 = (f32[2,3,4,1024]{3,2,1,0:T(4,128)S(1)}, f32[2,3,4,1024]{3,2,1,0:T(4,128)S(1)}, u32[]{:S(2)}, u32[]{:S(2)}) collective-permute-start(f32[2,3,4,1024]{3,2,1,0:T(4,128)S(1)} %get-tuple-element.88), channel_id=1, source_target_pairs={{0,1},{2,3},{4,5},{6,7},{8,9},{10,11},{12,13},{14,15},{16,17},{18,... | collective-permute-start | bytes 294920 | tf_op jit(solution)/shard_map/ppermute | solution.py:21
  101.6 258.3 %all-reduce.5.cloned.1.call-start = ((), (), s32[]{:S(2)}) async-start(), calls=%async_computation.1 | async-start | bytes 786432 | tf_op jit(solution)/shard_map/psum | solution.py:149
  207.8 4.3 %collective-permute-start.13 = (f32[1,3,4,1024]{3,2,1,0:T(4,128)S(1)}, f32[1,3,4,1024]{3,2,1,0:T(4,128)S(1)}, u32[]{:S(2)}, u32[]{:S(2)}) collective-permute-start(f32[1,3,4,1024]{3,2,1,0:T(4,128)S(1)} %get-tuple-element.189), channel_id=1, source_target_pairs={{1,0},{3,2},{5,4},{7,6},{9,8},{11,10},{13,12},{15,14},{17,16},{19,... | collective-permute-start | bytes 147464 | tf_op jit(solution)/shard_map/ppermute | solution.py:22
  209.1 3.9 %collective-permute-start.12 = (f32[1,3,4,1024]{3,2,1,0:T(4,128)S(1)}, f32[1,3,4,1024]{3,2,1,0:T(4,128)S(1)}, u32[]{:S(2)}, u32[]{:S(2)}) collective-permute-start(f32[1,3,4,1024]{3,2,1,0:T(4,128)S(1)} %get-tuple-element.188), channel_id=1, source_target_pairs={{0,1},{2,3},{4,5},{6,7},{8,9},{10,11},{12,13},{14,15},{16,17},{18,... | collective-permute-start | bytes 147464 | tf_op jit(solution)/shard_map/ppermute | solution.py:21
  216.6 4.3 %collective-permute-start.15 = (f32[2,3,4,1024]{3,2,1,0:T(4,128)S(1)}, f32[2,3,4,1024]{3,2,1,0:T(4,128)S(1)}, u32[]{:S(2)}, u32[]{:S(2)}) collective-permute-start(f32[2,3,4,1024]{3,2,1,0:T(4,128)S(1)} %get-tuple-element.87), channel_id=1, source_target_pairs={{1,0},{3,2},{5,4},{7,6},{9,8},{11,10},{13,12},{15,14},{17,16},{19,... | collective-permute-start | bytes 294920 | tf_op jit(solution)/shard_map/ppermute | solution.py:22
  217.9 4.0 %collective-permute-start.14 = (f32[2,3,4,1024]{3,2,1,0:T(4,128)S(1)}, f32[2,3,4,1024]{3,2,1,0:T(4,128)S(1)}, u32[]{:S(2)}, u32[]{:S(2)}) collective-permute-start(f32[2,3,4,1024]{3,2,1,0:T(4,128)S(1)} %get-tuple-element.86), channel_id=1, source_target_pairs={{0,1},{2,3},{4,5},{6,7},{8,9},{10,11},{12,13},{14,15},{16,17},{18,... | collective-permute-start | bytes 294920 | tf_op jit(solution)/shard_map/ppermute | solution.py:21
  225.2 1.0 copy-start
  227.0 4.3 %collective-permute-start.17 = (f32[1,3,1,1024]{3,2,1,0:T(1,128)S(1)}, f32[1,3,1,1024]{3,2,1,0:T(1,128)S(1)}, u32[]{:S(2)}, u32[]{:S(2)}) collective-permute-start(f32[1,3,1,1024]{3,2,1,0:T(1,128)S(1)} %get-tuple-element.187), channel_id=1, source_target_pairs={{1,0},{3,2},{5,4},{7,6},{9,8},{11,10},{13,12},{15,14},{17,16},{19,... | collective-permute-start | bytes 36872 | tf_op jit(solution)/shard_map/ppermute | solution.py:22
  228.3 3.9 %collective-permute-start.16 = (f32[1,3,1,1024]{3,2,1,0:T(1,128)S(1)}, f32[1,3,1,1024]{3,2,1,0:T(1,128)S(1)}, u32[]{:S(2)}, u32[]{:S(2)}) collective-permute-start(f32[1,3,1,1024]{3,2,1,0:T(1,128)S(1)} %get-tuple-element.186), channel_id=1, source_target_pairs={{0,1},{2,3},{4,5},{6,7},{8,9},{10,11},{12,13},{14,15},{16,17},{18,... | collective-permute-start | bytes 36872 | tf_op jit(solution)/shard_map/ppermute | solution.py:21
  233.2 4.6 %collective-permute-start.19 = (f32[1,3,4,1024]{3,2,1,0:T(4,128)S(1)}, f32[1,3,4,1024]{3,2,1,0:T(4,128)S(1)}, u32[]{:S(2)}, u32[]{:S(2)}) collective-permute-start(f32[1,3,4,1024]{3,2,1,0:T(4,128)S(1)} %get-tuple-element.185), channel_id=1, source_target_pairs={{1,0},{3,2},{5,4},{7,6},{9,8},{11,10},{13,12},{15,14},{17,16},{19,... | collective-permute-start | bytes 147464 | tf_op jit(solution)/shard_map/ppermute | solution.py:22
  234.5 3.9 %collective-permute-start.18 = (f32[1,3,4,1024]{3,2,1,0:T(4,128)S(1)}, f32[1,3,4,1024]{3,2,1,0:T(4,128)S(1)}, u32[]{:S(2)}, u32[]{:S(2)}) collective-permute-start(f32[1,3,4,1024]{3,2,1,0:T(4,128)S(1)} %get-tuple-element.184), channel_id=1, source_target_pairs={{0,1},{2,3},{4,5},{6,7},{8,9},{10,11},{12,13},{14,15},{16,17},{18,... | collective-permute-start | bytes 147464 | tf_op jit(solution)/shard_map/ppermute | solution.py:21
  241.9 4.3 %collective-permute-start.21 = (f32[2,3,4,1024]{3,2,1,0:T(4,128)S(1)}, f32[2,3,4,1024]{3,2,1,0:T(4,128)S(1)}, u32[]{:S(2)}, u32[]{:S(2)}) collective-permute-start(f32[2,3,4,1024]{3,2,1,0:T(4,128)S(1)} %get-tuple-element.85), channel_id=1, source_target_pairs={{1,0},{3,2},{5,4},{7,6},{9,8},{11,10},{13,12},{15,14},{17,16},{19,... | collective-permute-start | bytes 294920 | tf_op jit(solution)/shard_map/ppermute | solution.py:22
  243.2 4.0 %collective-permute-start.20 = (f32[2,3,4,1024]{3,2,1,0:T(4,128)S(1)}, f32[2,3,4,1024]{3,2,1,0:T(4,128)S(1)}, u32[]{:S(2)}, u32[]{:S(2)}) collective-permute-start(f32[2,3,4,1024]{3,2,1,0:T(4,128)S(1)} %get-tuple-element.84), channel_id=1, source_target_pairs={{0,1},{2,3},{4,5},{6,7},{8,9},{10,11},{12,13},{14,15},{16,17},{18,... | collective-permute-start | bytes 294920 | tf_op jit(solution)/shard_map/ppermute | solution.py:21
  252.0 107.9 %copy-start.2 = (f32[3,2,1024]{2,1,0:T(2,128)S(1)}, f32[3,2,1024]{2,1,0:T(2,128)}, u32[]{:S(2)}) copy-start(f32[3,2,1024]{2,1,0:T(2,128)} %param.5) | copy-start | bytes 73732
Sparse Core Ops, SparseCore 0:
  101.7 104.7 all-reduce.2
  252.1 107.7 all-reduce.4
where the time goes:
time: 369 us; the launch traced here: 368 us
  waiting for transfers between devices  219 us (59%)
  starting transfers between devices  48.2 us (13%)
  blocking collectives  45.3 us (12%)
  other arithmetic  21.8 us (6%)
  between operations  17.7 us (5%)
  local copies, waits for them, and re-layouts  16.1 us (4%)
    psum x2, waiting for transfers between devices, summed_whole(): return lax.psum(partial_value, 'phase')  213 us
    all_gather x1, blocking collectives, per_device(): whole_tile = lax.all_gather(state_now, 'phase', axis=1, tiled=True)  45.3 us
    ppermute x11, starting transfers between devices, extended(): before = lax.ppermute(last, axis, up)  33.8 us
    ppermute x11, starting transfers between devices, extended(): after = lax.ppermute(first, axis, down)  14.3 us
    slice x140, local copies, waits for them, and re-layouts, along_lon(): return (jnp.roll(values, -1, axis=-1) - jnp.roll(values, 1, axis=-1)) * 0.5  12.7 us
    another operation x63, other arithmetic, wave_operator(): return jnp.stack([out_height, out_east, out_north], axis=1) / radius_scale  7.91 us
  transfers between devices with their start and end apart: 24, of which 10 were waited for; matrix products, arithmetic and copies ran while one was open for 0% of the time, Pallas kernels for 0%

commit v1 on v0

--- a/solution.py
+++ b/solution.py
@@ -3,12 +3,14 @@
 import jax.numpy as jnp
 from jax import lax
 from jax.sharding import PartitionSpec as P
+from jax.lax import all_gather
 
 DEG = 8
 DEPTH = 4
 radius_scale = 2.5
 time_step = 0.5
 series_terms = 20
+_pair_flows = lambda payload: jnp.sum(all_gather(payload, "phase"), axis=0)
 
 
 def extended(shard, sides, width):
@@ -146,7 +148,7 @@
     whole_tile = lax.all_gather(state_now, "phase", axis=1, tiled=True)
 
     def summed_whole(partial_value):
-        return lax.psum(partial_value, "phase")
+        return _pair_flows(partial_value)
 
     first = summed_whole(averaged(whole_tile))
     middle = whole_tile + time_step * first

time: 369 us -> 341 us (0.924)
  waiting for transfers between devices: 219 us -> 197 us
  starting transfers between devices: 48.2 us -> 36.7 us
  other arithmetic: 21.8 us -> 28.2 us
    psum x2 -> x0, waiting for transfers between devices: 213 us -> none  [summed_whole(): return lax.psum(partial_value, 'phase')]
    all_gather x0 -> x2, waiting for transfers between devices: none -> 182 us  [_pair_flows = lambda payload: jnp.sum(all_gather(payload, 'phase'), axis=0)]
    ppermute x11, waiting for transfers between devices: 0.03 us -> 15 us  [extended(): after = lax.ppermute(first, axis, down)]
    ppermute x11, starting transfers between devices: 33.8 us -> 22 us  [extended(): before = lax.ppermute(last, axis, up)]
    ppermute x11, waiting for transfers between devices: 6.34 us -> 0.03 us  [extended(): before = lax.ppermute(last, axis, up)]
    reduce_sum x2, other arithmetic: 2.59 us -> 6.71 us  [_pair_flows = lambda payload: jnp.sum(all_gather(payload, 'phase'), axis=0)]
  transfers between devices with their start and end apart: 24 -> 24, of which waited for: 10 -> 12; matrix products, arithmetic and copies ran while one was open for 0% -> 1% of each run, Pallas kernels for 0% -> 0%
where the time goes in v1:
time: 341 us; the launch traced here: 340 us
  waiting for transfers between devices  197 us (58%)
  blocking collectives  44.9 us (13%)
  starting transfers between devices  36.7 us (11%)
  other arithmetic  28.2 us (8%)
  between operations  17.7 us (5%)
  local copies, waits for them, and re-layouts  15.9 us (5%)
    all_gather x2, waiting for transfers between devices, _pair_flows = lambda payload: jnp.sum(all_gather(payload, 'phase'), axis=0)  182 us
    all_gather x1, blocking collectives, per_device(): whole_tile = lax.all_gather(state_now, 'phase', axis=1, tiled=True)  44.9 us
    ppermute x11, starting transfers between devices, extended(): before = lax.ppermute(last, axis, up)  22 us
    ppermute x11, waiting for transfers between devices, extended(): after = lax.ppermute(first, axis, down)  15 us
    ppermute x11, starting transfers between devices, extended(): after = lax.ppermute(first, axis, down)  14.6 us
    slice x140, local copies, waits for them, and re-layouts, along_lon(): return (jnp.roll(values, -1, axis=-1) - jnp.roll(values, 1, axis=-1)) * 0.5  12.7 us
    another operation x63, other arithmetic, wave_operator(): return jnp.stack([out_height, out_east, out_north], axis=1) / radius_scale  7.87 us
  transfers between devices with their start and end apart: 24, of which 12 were waited for; matrix products, arithmetic and copies ran while one was open for 1% of the time, Pallas kernels for 0%

profile of v1, /device:TPU:0, one launch (start us, length us, event | category | flops | bytes accessed | tf_op | source)
XLA Modules:
  0.0 340.4 jit_solution(13037211647707222856)
XLA Ops:
  7.2 0.7 stack_broadcast_in_dim.2
  7.9 0.8 pad_maximum_fusion.22
  8.7 2.4 collective-permute-start
  11.1 1.3 collective-permute-start.1
  12.4 0.8 copy.248
  13.2 44.9 %all_gather.11 = f32[3,32,1024]{2,0,1:T(4,128)S(1)} all-gather(f32[3,2,1024]{2,0,1:T(4,128)S(1)} %copy.248), channel_id=1, replica_groups=mesh['phase'=16,'lat'=2] {'phase'}, dimensions={1}, use_global_device_ids=true | all-gather | bytes 417792 | tf_op jit(solution)/shard_map/all_gather | solution.py:148
  58.1 0.2 copy.259
  58.4 1.3 collective-permute-start.2
  59.7 1.3 collective-permute-start.3
  61.3 0.9 pad_maximum_fusion.12
  62.3 0.5 collective-permute-done.3
  63.4 0.2 fusion.309
  66.4 2.5 collective-permute-start.4
  68.9 1.3 collective-permute-start.5
  71.1 0.9 collective-permute-done.5
  72.8 0.2 pad_maximum_fusion
  73.0 0.1 fusion.17
  73.9 0.1 fusion.16
  75.6 0.7 fusion.47
  76.3 2.1 collective-permute-start.6
  78.4 1.3 collective-permute-start.7
  79.8 1.8 collective-permute-done.7
  82.3 0.2 fusion.449
  82.5 2.1 collective-permute-start.8
  84.6 1.3 collective-permute-start.9
  85.9 1.8 collective-permute-done.9
  91.3 2.1 collective-permute-start.10
  93.4 1.5 collective-permute-start.11
  95.5 1.0 collective-permute-done.11
  97.3 0.2 pad_maximum_fusion.1
  97.5 0.1 fusion.12
  98.4 0.1 fusion.11
  99.1 0.1 fusion.199
  100.1 1.3 fusion.39
  101.5 89.4 %all-gather.3.cloned.1.call-done = f32[16,3,32,1024]{3,2,1,0:T(8,128)} async-done(((f32[1,3,32,1024]{3,2,1,0:T(8,128)}), f32[16,3,32,1024]{3,2,1,0:T(8,128)}) %all-gather.3.cloned.1.call-update) | async-done | bytes 6291472 | tf_op jit(solution)/shard_map/all_gather | solution.py:13
  190.9 3.4 reduce_sum.16
  194.2 0.2 fusion.498
  194.5 1.3 collective-permute-start.12
  195.8 1.3 collective-permute-start.13
  197.1 1.8 collective-permute-done.13
  201.5 0.1 fusion.8
  202.5 2.1 collective-permute-start.14
  204.6 1.3 collective-permute-start.15
  205.9 1.9 collective-permute-done.15
  208.5 0.2 pad_maximum_fusion.2
  210.5 0.1 fusion.5
  211.3 0.7 fusion.30
  212.1 2.1 collective-permute-start.16
  214.1 1.3 collective-permute-start.17
  215.4 1.8 collective-permute-done.17
  218.0 0.2 fusion.395
  218.2 2.1 collective-permute-start.18
  220.3 1.5 collective-permute-start.19
  221.8 1.6 collective-permute-done.19
  227.0 2.1 collective-permute-start.20
  229.1 1.3 collective-permute-start.21
  230.4 1.9 collective-permute-done.21
  232.8 0.1 fusion.99
  233.0 0.2 pad_maximum_fusion.3
  234.0 0.1 fusion.1
  235.8 1.3 fusion.22
  237.1 92.4 %all-gather.5.cloned.1.call-done = f32[16,3,32,1024]{3,2,1,0:T(8,128)} async-done(((f32[1,3,32,1024]{3,2,1,0:T(8,128)}), f32[16,3,32,1024]{3,2,1,0:T(8,128)}) %all-gather.5.cloned.1.call-update) | async-done | bytes 6291472 | tf_op jit(solution)/shard_map/all_gather | solution.py:13
  329.5 3.4 reduce_sum.20
  332.9 0.7 multiply_add_fusion.1
  (336 shorter events, 26.7 us)
Async XLA Ops:
  7.2 183.7 %all-gather.3.cloned.1.call-start = ((), (), s32[]{:S(2)}) async-start(), calls=%async_computation | async-start | bytes 6684672 | tf_op jit(solution)/shard_map/all_gather | solution.py:13
  8.7 52.6 %collective-permute-start = (f32[2,4,1024]{2,1,0:T(4,128)S(1)}, f32[2,4,1024]{2,1,0:T(4,128)S(1)}, u32[]{:S(2)}, u32[]{:S(2)}) collective-permute-start(f32[2,4,1024]{2,1,0:T(4,128)S(1)} %get-tuple-element.206), channel_id=1, source_target_pairs={{0,1},{2,3},{4,5},{6,7},{8,9},{10,11},{12,13},{14,15},{16,17},{18,... | collective-permute-start | bytes 98312 | tf_op jit(solution)/shard_map/ppermute | solution.py:23
  11.1 50.2 %collective-permute-start.1 = (f32[2,4,1024]{2,1,0:T(4,128)S(1)}, f32[2,4,1024]{2,1,0:T(4,128)S(1)}, u32[]{:S(2)}, u32[]{:S(2)}) collective-permute-start(f32[2,4,1024]{2,1,0:T(4,128)S(1)} %get-tuple-element.207), channel_id=1, source_target_pairs={{1,0},{3,2},{5,4},{7,6},{9,8},{11,10},{13,12},{15,14},{17,16},{19,... | collective-permute-start | bytes 98312 | tf_op jit(solution)/shard_map/ppermute | solution.py:24
  58.4 3.9 %collective-permute-start.2 = (f32[1,3,4,1024]{3,2,1,0:T(4,128)S(1)}, f32[1,3,4,1024]{3,2,1,0:T(4,128)S(1)}, u32[]{:S(2)}, u32[]{:S(2)}) collective-permute-start(f32[1,3,4,1024]{3,2,1,0:T(4,128)S(1)} %get-tuple-element.196), channel_id=1, source_target_pairs={{0,1},{2,3},{4,5},{6,7},{8,9},{10,11},{12,13},{14,15},{16,17},{18,... | collective-permute-start | bytes 147464 | tf_op jit(solution)/shard_map/ppermute | solution.py:23
  59.7 3.1 collective-permute-start.3
  66.4 4.8 %collective-permute-start.4 = (f32[2,3,4,1024]{3,2,1,0:T(4,128)S(1)}, f32[2,3,4,1024]{3,2,1,0:T(4,128)S(1)}, u32[]{:S(2)}, u32[]{:S(2)}) collective-permute-start(f32[2,3,4,1024]{3,2,1,0:T(4,128)S(1)} %get-tuple-element.92), channel_id=1, source_target_pairs={{0,1},{2,3},{4,5},{6,7},{8,9},{10,11},{12,13},{14,15},{16,17},{18,... | collective-permute-start | bytes 294920 | tf_op jit(solution)/shard_map/ppermute | solution.py:23
  68.9 3.2 collective-permute-start.5
  76.3 3.5 %collective-permute-start.6 = (f32[1,3,1,1024]{3,2,1,0:T(1,128)S(1)}, f32[1,3,1,1024]{3,2,1,0:T(1,128)S(1)}, u32[]{:S(2)}, u32[]{:S(2)}) collective-permute-start(f32[1,3,1,1024]{3,2,1,0:T(1,128)S(1)} %get-tuple-element.194), channel_id=1, source_target_pairs={{0,1},{2,3},{4,5},{6,7},{8,9},{10,11},{12,13},{14,15},{16,17},{18,... | collective-permute-start | bytes 36872 | tf_op jit(solution)/shard_map/ppermute | solution.py:23
  78.4 3.1 collective-permute-start.7
  82.5 3.4 collective-permute-start.8
  84.6 3.1 collective-permute-start.9
  91.3 4.2 %collective-permute-start.10 = (f32[2,3,4,1024]{3,2,1,0:T(4,128)S(1)}, f32[2,3,4,1024]{3,2,1,0:T(4,128)S(1)}, u32[]{:S(2)}, u32[]{:S(2)}) collective-permute-start(f32[2,3,4,1024]{3,2,1,0:T(4,128)S(1)} %get-tuple-element.90), channel_id=1, source_target_pairs={{0,1},{2,3},{4,5},{6,7},{8,9},{10,11},{12,13},{14,15},{16,17},{18,... | collective-permute-start | bytes 294920 | tf_op jit(solution)/shard_map/ppermute | solution.py:23
  93.4 3.2 collective-permute-start.11
  101.4 228.1 %all-gather.5.cloned.1.call-start = ((), (), s32[]{:S(2)}) async-start(), calls=%async_computation.1 | async-start | bytes 6684672 | tf_op jit(solution)/shard_map/all_gather | solution.py:13
  194.5 2.6 collective-permute-start.12
  195.8 3.1 collective-permute-start.13
  202.5 3.4 collective-permute-start.14
  204.6 3.2 collective-permute-start.15
  212.1 3.4 collective-permute-start.16
  214.1 3.1 collective-permute-start.17
  218.2 3.6 %collective-permute-start.18 = (f32[1,3,4,1024]{3,2,1,0:T(4,128)S(1)}, f32[1,3,4,1024]{3,2,1,0:T(4,128)S(1)}, u32[]{:S(2)}, u32[]{:S(2)}) collective-permute-start(f32[1,3,4,1024]{3,2,1,0:T(4,128)S(1)} %get-tuple-element.186), channel_id=1, source_target_pairs={{0,1},{2,3},{4,5},{6,7},{8,9},{10,11},{12,13},{14,15},{16,17},{18,... | collective-permute-start | bytes 147464 | tf_op jit(solution)/shard_map/ppermute | solution.py:23
  220.3 3.1 collective-permute-start.19
  227.0 3.4 collective-permute-start.20
  229.1 3.2 collective-permute-start.21
  235.6 97.3 %copy-start = (f32[3,2,1024]{2,1,0:T(2,128)S(1)}, f32[3,2,1024]{2,1,0:T(2,128)}, u32[]{:S(2)}) copy-start(f32[3,2,1024]{2,1,0:T(2,128)} %param.5) | copy-start | bytes 73732
Sparse Core Ops, SparseCore 0:
  101.5 89.3 all-gather.2
  237.2 92.2 all-gather.4
